TPU v7x, 32 devices: a whole 2x2x4 slice. The times are simulated.
32 devices in a mesh: section: 4 (over y, core), batch: 8 (over z, x).
Axes of the slice: x: 2, y: 2, z: 4, core: 2. Of those that a mesh axis runs over, the one named last changes fastest.
Arguments:
- masters: float32 [32, 512, 1024], P('section', 'batch'), may hold values from -0.1875 to 0.1875
- first_moment: float32 [32, 512, 1024], P('section', 'batch')
- second_moment: float32 [32, 512, 1024], P('section', 'batch')
- section_table: float32 [8, 6144], P('section'), may hold values from -1.2 to 1.2
- table_first: float32 [8, 6144], P('section')
- table_second: float32 [8, 6144], P('section')
- owners: int32 [29], replicated, may hold values from 0 to 31, as said below
- step_count: int32 [1], replicated, may hold values from 2 to 20
- phones: int32 [64, 512], P(('section', 'batch')), may hold values from 0 to 511
- codes: int32 [64, 512, 8], P(('section', 'batch')), may hold values from 0 to 1023
- segments: int32 [64, 512], P(('section', 'batch')), may hold values from 0 to 2, never falling along the last dimension, each value on 1 to 384 neighbouring positions
- sections: int32 [64, 1], P(('section', 'batch')), may hold values from 0 to 7
- targets: int32 [64, 512], P(('section', 'batch')), may hold values from 0 to 1023
Outputs:
- new_masters: float32 [32, 512, 1024], P('section', 'batch')
- new_first: float32 [32, 512, 1024], P('section', 'batch')
- new_second: float32 [32, 512, 1024], P('section', 'batch')
- new_table: float32 [8, 6144], P('section')
- new_table_first: float32 [8, 6144], P('section')
- new_table_second: float32 [8, 6144], P('section')
- grad_norm: float32 [], replicated
- loss: float32 [], replicated
Inputs may be any that keep to these rules, and one draw needn't show every extreme that they name: `owners`: distinct slot numbers; slot 0 and slot 31 are always among them; a section index of the slots owns a varying number of blocks. `sections`: every section is the section of some row; rows of one section may stand on any device.
All inputs are finite; a program needn't handle non-finite values.
Results may differ from a plain program's by a relative error of at most 0.0067.
Values may be sent and summed in bfloat16 or wider, within the bound.
A program may use at most 320 MiB of HBM per device.

v0:
```python
import math
import jax
import jax.numpy as jnp
from jax import lax
from jax.sharding import PartitionSpec as P

D = 1024
HEADS = 16
HD = 64
FF = 4096
CODES = 1024
LEVELS = 8
PHONES = 512
SECTIONS = 8
clip_limit = 0.002
learn_rate = 0.02
table_rate = 0.1
beta_one = 0.9
beta_two = 0.95
adam_eps = 1e-08
decay_rate = 0.1
norm_eps = 1e-05
pos_scale = 0.1
exact = lax.Precision.HIGHEST
float_out = jnp.float32


def positions(segs):
    index = jnp.broadcast_to(jnp.arange(segs.shape[-1], dtype=jnp.int32), segs.shape)
    first = jnp.ones(segs.shape[:-1] + (1,), dtype=bool)
    change = jnp.concatenate([first, segs[..., 1:] != segs[..., :-1]], axis=-1)
    starts = lax.cummax(jnp.where(change, index, jnp.zeros_like(index)), axis=segs.ndim - 1)
    return (index - starts).astype(jnp.float32)


def sinusoid(place, width):
    column = jnp.arange(width)
    rate = jnp.exp(-(2 * (column // 2)).astype(jnp.float32) * (math.log(10000.0) / width))
    angle = place[..., None] * rate
    return pos_scale * jnp.where(column % 2 == 0, jnp.sin(angle), jnp.cos(angle))


def normalize(stream):
    centred = stream - jnp.mean(stream, axis=-1, keepdims=True)
    scale = lax.rsqrt(jnp.mean(centred * centred, axis=-1, keepdims=True) + norm_eps)
    return (centred * scale, scale)


def norm_back(grad, normed, scale, gain):
    inner = grad * (1.0 + gain)
    result = scale * (
        inner
        - jnp.mean(inner, axis=-1, keepdims=True)
        - normed * jnp.mean(inner * normed, axis=-1, keepdims=True)
    )
    return (result, jnp.sum(grad * normed, axis=1), jnp.sum(grad, axis=1))


def unpack(blocks):
    half = blocks.shape[1]
    width = blocks.shape[2]
    code_w = blocks[0:2].reshape(2 * half, width)
    phone_w = blocks[2]
    head_w = blocks[3:5].reshape(width, 2 * half)
    qkv_w = blocks[5:11].reshape(3, width, width)
    out_w = blocks[11:13].reshape(width, width)
    up_w = blocks[13:21].reshape(4, width, width)
    down_w = blocks[21:29].reshape(4 * width, width)
    return (code_w, phone_w, head_w, qkv_w, out_w, up_w, down_w)


def pack(pieces, half, width):
    return jnp.concatenate([piece.reshape(-1, half, width) for piece in pieces], axis=0)


def attend_scores(queries, key_vecs, same):
    scores = jnp.einsum(
        "rlhe,rmhe->rhlm", queries, key_vecs, preferred_element_type=float_out
    ) * HD ** (-0.5)
    return jnp.where(same[:, None], scores, -1000000000.0)


def forward(matrices, params, phones, codes, segments, section_ids, targets, section_hot):
    code_w, phone_w, head_w, qkv_w, out_w, up_w, down_w = matrices
    rows, length = segments.shape
    levels = (jnp.arange(LEVELS)[None, :] <= section_ids[:, None]).astype(jnp.bfloat16)
    vocab = jnp.arange(CODES)
    multi = jnp.zeros((rows, length, CODES), jnp.bfloat16)
    for level in range(LEVELS):
        multi = (
            multi
            + (codes[:, :, level, None] == vocab).astype(jnp.bfloat16)
            * levels[:, level, None, None]
        )
    phone_hot = (phones[:, :, None] == jnp.arange(PHONES)).astype(jnp.bfloat16)
    stream = jnp.einsum("rlc,cd->rld", multi, code_w, preferred_element_type=float_out)
    stream = stream + jnp.einsum(
        "rlp,pd->rld", phone_hot, phone_w, preferred_element_type=float_out
    )
    stream = stream + sinusoid(positions(segments), D)
    normed_one, scale_one = normalize(stream)
    input_one = (normed_one * (1.0 + params[:, 0]) + params[:, 1]).astype(jnp.bfloat16)
    qkv = jnp.einsum("rld,kde->krle", input_one, qkv_w, preferred_element_type=float_out).astype(
        jnp.bfloat16
    )
    heads = qkv.reshape(3, rows, length, HEADS, HD)
    same = segments[:, :, None] == segments[:, None, :]
    scores = attend_scores(heads[0], heads[1], same)
    log_total = jax.nn.logsumexp(scores, axis=-1)
    probs = jnp.exp(scores - log_total[..., None]).astype(jnp.bfloat16)
    mixed = jnp.einsum("rhlm,rmhe->rlhe", probs, heads[2], preferred_element_type=float_out)
    mixed = mixed.astype(jnp.bfloat16).reshape(rows, length, D)
    stream = stream + jnp.einsum("rld,de->rle", mixed, out_w, preferred_element_type=float_out)
    normed_two, scale_two = normalize(stream)
    input_two = (normed_two * (1.0 + params[:, 2]) + params[:, 3]).astype(jnp.bfloat16)
    hidden = jnp.einsum("rld,gde->rlge", input_two, up_w, preferred_element_type=float_out)
    active = jax.nn.gelu(hidden, approximate=False).astype(jnp.bfloat16).reshape(rows, length, FF)
    stream = stream + jnp.einsum("rlf,fd->rld", active, down_w, preferred_element_type=float_out)
    normed_three, scale_three = normalize(stream)
    input_three = (normed_three * (1.0 + params[:, 4]) + params[:, 5]).astype(jnp.bfloat16)
    logits = jnp.einsum("rld,dc->rlc", input_three, head_w, preferred_element_type=float_out)
    log_norm = jax.nn.logsumexp(logits, axis=-1)
    target_hot = (targets[:, :, None] == vocab).astype(jnp.float32)
    losses = log_norm - jnp.sum(logits * target_hot, axis=-1)
    section_loss = jnp.sum(section_hot * jnp.sum(losses, axis=1)[:, None], axis=0)
    kept = (
        multi,
        phone_hot,
        normed_one,
        scale_one,
        input_one,
        heads,
        same,
        log_total,
        mixed,
        normed_two,
        scale_two,
        input_two,
        hidden,
        active,
        normed_three,
        scale_three,
        input_three,
        logits,
        log_norm,
        target_hot,
    )
    return (kept, section_loss)


def backward(matrices, params, kept, row_weight):
    code_w, phone_w, head_w, qkv_w, out_w, up_w, down_w = matrices
    (
        multi,
        phone_hot,
        normed_one,
        scale_one,
        input_one,
        heads,
        same,
        log_total,
        mixed,
        normed_two,
        scale_two,
        input_two,
        hidden,
        active,
        normed_three,
        scale_three,
        input_three,
        logits,
        log_norm,
        target_hot,
    ) = kept
    rows, length = (same.shape[0], same.shape[1])
    predicted = jnp.exp(logits - log_norm[..., None])
    grad_logits = ((predicted - target_hot) * row_weight[:, None, None]).astype(jnp.bfloat16)
    grad_head = jnp.einsum(
        "rld,rlc->dc", input_three, grad_logits, preferred_element_type=float_out
    )
    grad_three = jnp.einsum("rlc,dc->rld", grad_logits, head_w, preferred_element_type=float_out)
    grad_stream, gain_three, shift_three = norm_back(
        grad_three, normed_three, scale_three, params[:, 4]
    )
    grad_ffn = grad_stream.astype(jnp.bfloat16)
    grad_down = jnp.einsum("rlf,rld->fd", active, grad_ffn, preferred_element_type=float_out)
    grad_active = jnp.einsum("rld,fd->rlf", grad_ffn, down_w, preferred_element_type=float_out)
    _, gelu_pull = jax.vjp(lambda value: jax.nn.gelu(value, approximate=False), hidden)
    grad_hidden = gelu_pull(grad_active.reshape(hidden.shape))[0].astype(jnp.bfloat16)
    grad_up = jnp.einsum("rld,rlge->gde", input_two, grad_hidden, preferred_element_type=float_out)
    grad_two = jnp.einsum("rlge,gde->rld", grad_hidden, up_w, preferred_element_type=float_out)
    grad_norm_two, gain_two, shift_two = norm_back(grad_two, normed_two, scale_two, params[:, 2])
    grad_stream = grad_stream + grad_norm_two
    grad_attn = grad_stream.astype(jnp.bfloat16)
    grad_out = jnp.einsum("rld,rle->de", mixed, grad_attn, preferred_element_type=float_out)
    grad_mixed = jnp.einsum("rle,de->rld", grad_attn, out_w, preferred_element_type=float_out)
    grad_mixed = grad_mixed.astype(jnp.bfloat16).reshape(rows, length, HEADS, HD)
    scores = attend_scores(heads[0], heads[1], same)
    probs = jnp.exp(scores - log_total[..., None])
    probs_low = probs.astype(jnp.bfloat16)
    grad_values = jnp.einsum(
        "rhlm,rlhe->rmhe", probs_low, grad_mixed, preferred_element_type=float_out
    )
    grad_probs = jnp.einsum(
        "rlhe,rmhe->rhlm", grad_mixed, heads[2], preferred_element_type=float_out
    )
    grad_scores = (
        probs * (grad_probs - jnp.sum(probs * grad_probs, axis=-1, keepdims=True))
    ).astype(jnp.bfloat16)
    grad_queries = jnp.einsum(
        "rhlm,rmhe->rlhe", grad_scores, heads[1], preferred_element_type=float_out
    ) * HD ** (-0.5)
    grad_key_vecs = jnp.einsum(
        "rhlm,rlhe->rmhe", grad_scores, heads[0], preferred_element_type=float_out
    ) * HD ** (-0.5)
    grad_qkv = (
        jnp.stack([grad_queries, grad_key_vecs, grad_values])
        .reshape(3, rows, length, D)
        .astype(jnp.bfloat16)
    )
    grad_proj = jnp.einsum("rld,krle->kde", input_one, grad_qkv, preferred_element_type=float_out)
    grad_one = jnp.einsum("krle,kde->rld", grad_qkv, qkv_w, preferred_element_type=float_out)
    grad_norm_one, gain_one, shift_one = norm_back(grad_one, normed_one, scale_one, params[:, 0])
    grad_embed = (grad_stream + grad_norm_one).astype(jnp.bfloat16)
    grad_code = jnp.einsum("rlc,rld->cd", multi, grad_embed, preferred_element_type=float_out)
    grad_phone = jnp.einsum("rlp,rld->pd", phone_hot, grad_embed, preferred_element_type=float_out)
    half = phone_w.shape[0]
    block_grads = pack(
        (grad_code, grad_phone, grad_head, grad_proj, grad_out, grad_up, grad_down), half, D
    )
    row_grads = jnp.stack(
        [gain_one, shift_one, gain_two, shift_two, gain_three, shift_three], axis=1
    )
    return (block_grads, row_grads)


def adam(weight, first, second, grad, rate, step):
    new_first = beta_one * first + (1.0 - beta_one) * grad
    new_second = beta_two * second + (1.0 - beta_two) * grad * grad
    fix_one = 1.0 - jnp.power(beta_one, step)
    fix_two = 1.0 - jnp.power(beta_two, step)
    update = new_first / fix_one / (jnp.sqrt(new_second / fix_two) + adam_eps)
    return (weight - rate * (update + decay_rate * weight), new_first, new_second)


def per_device(
    masters,
    first_moment,
    second_moment,
    section_table,
    table_first,
    table_second,
    owners,
    step_count,
    phones,
    codes,
    segments,
    sections,
    targets,
):
    section_width = lax.axis_size("section")
    batch_width = lax.axis_size("batch")
    section_ids = sections[:, 0]
    row_count = section_ids.shape[0]
    section_hot = (section_ids[:, None] == jnp.arange(SECTIONS)[None, :]).astype(jnp.float32)
    local_counts = jnp.sum(section_hot, axis=0) * segments.shape[1]
    shard_rows = lax.all_gather(masters.astype(jnp.bfloat16), "batch", axis=1, tiled=True)
    all_slots = lax.all_gather(shard_rows, "section", axis=0, tiled=True)
    blocks = jnp.take(all_slots, owners, axis=0)
    table = lax.all_gather(section_table, "section", axis=0, tiled=True)
    matrices = unpack(blocks)
    params = jnp.einsum("rs,sk->rk", section_hot, table, precision=exact).reshape(
        row_count, 6, 1, D
    )
    kept, section_loss = forward(
        matrices, params, phones, codes, segments, section_ids, targets, section_hot
    )
    counts, loss_sums = lax.psum((local_counts, section_loss), ("section", "batch"))
    row_weight = jnp.sum(section_hot / (SECTIONS * counts)[None, :], axis=1)
    block_grads, row_grads = backward(matrices, params, kept, row_weight)
    table_local = jnp.einsum(
        "rs,rk->sk", section_hot, row_grads.reshape(row_count, 6 * D), precision=exact
    )
    table_sum = lax.psum(table_local, ("section", "batch"))
    own_count = section_table.shape[0]
    table_grad = lax.dynamic_slice_in_dim(
        table_sum, lax.axis_index("section") * own_count, own_count, 0
    )
    per_group = masters.shape[0]
    piece_rows = masters.shape[1]
    split_grads = block_grads.reshape(block_grads.shape[0], batch_width, piece_rows, D)
    group_of = owners // per_group
    within = owners % per_group
    target_slot = (
        (group_of * batch_width)[:, None] * per_group
        + jnp.arange(batch_width)[None, :] * per_group
        + within[:, None]
    )
    arranged = jnp.zeros((section_width * batch_width * per_group, piece_rows, D), jnp.float32)
    arranged = arranged.at[target_slot.reshape(-1)].set(split_grads.reshape(-1, piece_rows, D))
    own_grad = lax.psum_scatter(arranged, ("section", "batch"), scatter_dimension=0, tiled=True)
    square_sum = jnp.sum(own_grad * own_grad) + jnp.sum(table_grad * table_grad) / batch_width
    grad_norm = jnp.sqrt(lax.psum(square_sum, ("section", "batch")))
    clip_factor = jnp.minimum(1.0, clip_limit / grad_norm)
    step = step_count[0].astype(jnp.float32)
    new_masters, new_first, new_second = adam(
        masters, first_moment, second_moment, own_grad * clip_factor, learn_rate, step
    )
    new_table, new_table_first, new_table_second = adam(
        section_table, table_first, table_second, table_grad * clip_factor, table_rate, step
    )
    loss = jnp.sum(loss_sums / (SECTIONS * counts))
    return (
        new_masters,
        new_first,
        new_second,
        new_table,
        new_table_first,
        new_table_second,
        grad_norm,
        loss,
    )


def solution(mesh):
    return jax.shard_map(
        per_device,
        mesh=mesh,
        in_specs=(
            P("section", "batch", None),
            P("section", "batch", None),
            P("section", "batch", None),
            P("section", None),
            P("section", None),
            P("section", None),
            P(),
            P(),
            P(("section", "batch"), None),
            P(("section", "batch"), None, None),
            P(("section", "batch"), None),
            P(("section", "batch"), None),
            P(("section", "batch"), None),
        ),
        out_specs=(
            P("section", "batch", None),
            P("section", "batch", None),
            P("section", "batch", None),
            P("section", None),
            P("section", None),
            P("section", None),
            P(),
            P(),
        ),
        check_vma=False,
    )
```

profile of v0, /device:TPU:0, one launch (start us, length us, event | category | flops | bytes accessed | tf_op | source)
XLA Modules:
  0.0 2446.3 jit_solution(5869725408270620591)
XLA Ops:
  7.2 2.7 convert_element_type.90
  10.0 128.4 %all-gather.4.cloned.1.call-done = bf16[8,512,1024]{2,1,0:T(8,128)(2,1)} async-done(((bf16[8,64,1024]{2,1,0:T(8,128)(2,1)}), bf16[8,512,1024]{2,1,0:T(8,128)(2,1)}) %all-gather.4.cloned.1.call-update) | async-done | bytes 8388624 | tf_op jit(solution)/shard_map/all_gather | solution.py:267
  139.2 38.7 %psum.28 = f32[8]{0:T(128)S(1)} all-reduce(f32[8]{0:T(128)S(1)} %broadcast_multiply_fusion.10), channel_id=1, replica_groups=mesh['section'=4,'batch'=8] {'section','batch'}, use_global_device_ids=true, to_apply=%region_13.14 | all-reduce | flops 8 | bytes 64 | tf_op jit(solution)/shard_map/psum | solution.py:278
  179.1 7.4 all-gather
  189.8 151.7 %all-gather.6.cloned.1.call-done = bf16[32,512,1024]{2,1,0:T(8,128)(2,1)} async-done(((bf16[8,512,1024]{2,1,0:T(8,128)(2,1)}), bf16[32,512,1024]{2,1,0:T(8,128)(2,1)}) %all-gather.6.cloned.1.call-update) | async-done | bytes 33554448 | tf_op jit(solution)/shard_map/all_gather | solution.py:268
  341.5 22.0 gather_fusion
  363.5 20.5 broadcast_select_fusion
  384.0 5.7 fusion.89
  389.7 3.5 slice.160
  393.2 14.0 fusion.88
  407.4 6.3 fusion.82
  413.7 17.8 fusion.92
  432.1 1.4 copy-done.47
  433.5 10.1 convert_bitcast_fusion
  443.6 3.3 fusion.90
  446.9 13.8 fusion
  460.7 14.1 exponential_reduce_fusion
  474.9 15.6 convolution_convert_fusion.2
  490.5 6.3 fusion.93
  497.4 49.3 %multiply_convert_fusion.1 = (bf16[2,512,4,1024]{3,1,2,0:T(8,128)(2,1)}, f32[2,512,4,1024]{3,1,2,0:T(8,128)}, f32[2,512,4,1024]{3,1,2,0:T(8,128)}) fusion(bf16[4,1024,1024,1]{2,1,0,3:T(8,128)(2,1)S(1)} %bitcast.258, f32[2,512,1024]{2,1,0:T(8,128)S(1)} %get-tuple-element.74, f32[2,1024]{1,0:T(2,128)S(1)} %get-tuple-element.95, ...), kind=kOutput, calls=%fused_computation.14 | convolution fusion | flops 8867807232 | bytes 54550528 | tf_op jit(solution)/shard_map/rld,gde->rlge/dot_general | solution.py:116
  546.7 11.4 copy.71
  558.1 14.7 fusion.94
  573.4 2.5 copy-done.28
  575.9 2.5 fusion.95
  578.5 1.6 select_reduce_fusion
  580.2 0.6 select_reduce_fusion.1
  580.9 4.0 multiply_reduce_fusion.1
  584.9 1.2 subtract_multiply_fusion
  586.1 24.3 add_convert_fusion
  610.4 16.0 fusion.12
  626.4 1.4 multiply_add_fusion
  627.8 2.0 copy-done.12
  629.8 3.7 convolution_convert_fusion.1
  633.5 2.9 copy.73
  636.5 25.7 %multiply_reduce_fusion = (f32[2,16,512]{2,1,0:T(8,128)S(1)}, f32[2,16,512,512]{2,3,1,0:T(8,128)}) fusion(f32[2,16,512,512]{2,3,1,0:T(8,128)} %get-tuple-element.72, f32[2,16,512]{2,1,0:T(8,128)S(1)} %copy-done.30, pred[2,512,512]{1,2,0:T(8,128)(4,1)S(1)} %copy-done.3, bf16[2,512,16,64]{1,3,2,0:T(8,128)(2,1)S(1)} %bitcast.243, ...), kind=kOutput, calls=%fused_computation.3 | convolution fusion | flops 1115668480 | bytes 71958528 | tf_op jit(solution)/shard_map/rlhe,rmhe->rhlm/dot_general | solution.py:204
  662.2 28.4 %multiply_convert_fusion = bf16[2,16,512,512]{2,3,1,0:T(8,128)(2,1)} fusion(f32[2,16,512,512]{2,3,1,0:T(8,128)} %get-tuple-element.83, f32[2,16,512,512]{2,3,1,0:T(8,128)} %get-tuple-element.72, f32[2,16,512]{2,1,0:T(8,128)S(1)} %get-tuple-element.82, f32[2,16,512]{2,1,0:T(8,128)S(1)} %copy-done.30, pred[2,512,512]{1,2,0:T(8,128)(4,1)S(1)} %copy-done.3), kind=kLoop, calls=%fused_computation.2 | loop fusion | flops 50331648 | bytes 84541440 | tf_op jit(solution)/shard_map/convert_element_type | solution.py:209
  690.6 9.9 multiply_convert_fusion.3
  700.5 13.0 multiply_convert_fusion.2
  713.5 16.2 convolution_convert_fusion
  729.7 23.3 fusion.76
  753.1 5.4 fusion.49
  758.4 2.4 copy.77
  760.9 4.1 copy.78
  765.0 3.9 copy.79
  769.0 14.8 fusion.23
  783.9 9.2 fusion.11
  793.2 0.9 fusion.60
  794.3 5.5 add_convert_fusion.1
  800.1 5.5 fusion.80
  805.6 2.3 constant_dynamic-update-slice_fusion.3
  807.9 2.6 bitcast_dynamic-update-slice_fusion.2
  810.5 2.3 constant_dynamic-update-slice_fusion.2
  812.8 12.1 constant_dynamic-update-slice_fusion.1
  824.9 4.3 bitcast_dynamic-update-slice_fusion.1
  829.2 13.1 constant_dynamic-update-slice_fusion
  842.3 12.3 bitcast_dynamic-update-slice_fusion
  854.6 21.3 broadcast_in_dim.44
  875.9 107.0 %scatter_fusion = f32[256,64,1024]{2,1,0:T(8,128)} fusion(f32[256,64,1024]{2,1,0:T(8,128)} %broadcast_in_dim.44, s32[232]{0:T(256)S(1)} %bitcast.280, f32[232,64,1024]{2,1,0:T(8,128)} %bitcast.238), kind=kCustom, calls=%fused_computation.1 | custom fusion | bytes 182453152 | tf_op jit(solution)/shard_map/scatter | solution.py:300
  983.8 1.6 multiply_reduce_fusion.10
  986.1 1399.5 %reduce-scatter.2.cloned.1.call-done = f32[8,64,1024]{2,1,0:T(8,128)} async-done(((f32[256,64,1024]{2,1,0:T(8,128)}), f32[8,64,1024]{2,1,0:T(8,128)}) %reduce-scatter.2.cloned.1.call-update) | async-done | bytes 2097168 | tf_op jit(solution)/shard_map/reduce_scatter | solution.py:301
  2385.6 2.7 multiply_reduce_fusion.9
  2389.0 39.4 %all-reduce.1 = (f32[]{:T(128)}, f32[8]{0:T(128)S(1)}) all-reduce(f32[]{:T(128)S(6)} %add.310, f32[8]{0:T(128)S(1)} %copy-done.99), channel_id=1, replica_groups=mesh['section'=4,'batch'=8] {'section','batch'}, use_global_device_ids=true, to_apply=%region_33.34 | all-reduce | flops 9 | bytes 72 | tf_op jit(solution)/shard_map/psum | solution.py:303
  2429.7 1.7 multiply_subtract_fusion.1
  2431.5 6.9 multiply_subtract_fusion
  (300 shorter events, 8.1 us)
Async XLA Ops:
  7.2 131.2 %all-gather.4.cloned.1.call-start = ((), (), s32[]{:S(2)}) async-start(), calls=%async_computation.1 | async-start | bytes 9437184 | tf_op jit(solution)/shard_map/all_gather | solution.py:267
  10.0 331.5 %all-gather.6.cloned.1.call-start = ((), (), s32[]{:S(2)}) async-start(), calls=%async_computation.2 | async-start | bytes 41943040 | tf_op jit(solution)/shard_map/all_gather | solution.py:268
  138.4 39.5 %copy-start.33 = (s32[2,512]{1,0:T(2,128)S(1)}, s32[2,512]{1,0:T(2,128)}, u32[]{:S(2)}) copy-start(s32[2,512]{1,0:T(2,128)} %param.23) | copy-start | bytes 12292
  138.4 40.7 %copy-start.31 = (f32[2,6144]{1,0:T(2,128)S(1)}, f32[2,6144]{1,0:T(2,128)}, u32[]{:S(2)}) copy-start(f32[2,6144]{1,0:T(2,128)} %param.16) | copy-start | bytes 147460
  138.4 48.6 %copy-start.103 = (s32[29]{0:T(128)S(1)}, s32[29]{0:T(128)}, u32[]{:S(2)}) copy-start(s32[29]{0:T(128)} %param.19) | copy-start | bytes 352
  138.4 50.1 %copy-start.42 = (s32[2,512,8]{1,2,0:T(8,128)S(1)}, s32[2,512,8]{1,2,0:T(8,128)}, u32[]{:S(2)}) copy-start(s32[2,512,8]{1,2,0:T(8,128)} %param.22) | copy-start | bytes 98308
  138.4 845.4 %all-reduce.4.cloned.1.call-start = ((), (), s32[]{:S(2)}) async-start(), calls=%async_computation.4 | async-start | bytes 393216 | tf_op jit(solution)/shard_map/psum | solution.py:284
  188.4 218.9 %copy-start.83 = (bf16[2]{0:T(256)(128)(2,1)}, bf16[2]{0:T(256)(128)(2,1)S(1)}, u32[]{:S(2)}) copy-start(bf16[2]{0:T(256)(128)(2,1)S(1)} %get-tuple-element.58) | copy-start | bytes 16
  188.4 218.9 %copy-start.85 = (bf16[2]{0:T(256)(128)(2,1)}, bf16[2]{0:T(256)(128)(2,1)S(1)}, u32[]{:S(2)}) copy-start(bf16[2]{0:T(256)(128)(2,1)S(1)} %get-tuple-element.59) | copy-start | bytes 16
  188.4 218.9 %copy-start.87 = (bf16[2]{0:T(256)(128)(2,1)}, bf16[2]{0:T(256)(128)(2,1)S(1)}, u32[]{:S(2)}) copy-start(bf16[2]{0:T(256)(128)(2,1)S(1)} %get-tuple-element.60) | copy-start | bytes 16
  188.4 218.9 %copy-start.89 = (bf16[2]{0:T(256)(128)(2,1)}, bf16[2]{0:T(256)(128)(2,1)S(1)}, u32[]{:S(2)}) copy-start(bf16[2]{0:T(256)(128)(2,1)S(1)} %get-tuple-element.61) | copy-start | bytes 16
  188.4 218.9 %copy-start.91 = (bf16[2]{0:T(256)(128)(2,1)}, bf16[2]{0:T(256)(128)(2,1)S(1)}, u32[]{:S(2)}) copy-start(bf16[2]{0:T(256)(128)(2,1)S(1)} %get-tuple-element.62) | copy-start | bytes 16
  188.4 218.9 %copy-start.93 = (bf16[2]{0:T(256)(128)(2,1)}, bf16[2]{0:T(256)(128)(2,1)S(1)}, u32[]{:S(2)}) copy-start(bf16[2]{0:T(256)(128)(2,1)S(1)} %get-tuple-element.63) | copy-start | bytes 16
  188.4 218.9 %copy-start.95 = (bf16[2]{0:T(256)(128)(2,1)}, bf16[2]{0:T(256)(128)(2,1)S(1)}, u32[]{:S(2)}) copy-start(bf16[2]{0:T(256)(128)(2,1)S(1)} %get-tuple-element.64) | copy-start | bytes 16
  188.4 218.9 %copy-start.97 = (bf16[2]{0:T(256)(128)(2,1)}, bf16[2]{0:T(256)(128)(2,1)S(1)}, u32[]{:S(2)}) copy-start(bf16[2]{0:T(256)(128)(2,1)S(1)} %get-tuple-element.65) | copy-start | bytes 16
  188.6 218.8 %copy-start.63 = (s32[2,512]{1,0:T(2,128)}, s32[2,512]{1,0:T(2,128)S(1)}, u32[]{:S(2)}) copy-start(s32[2,512]{1,0:T(2,128)S(1)} %get-tuple-element.85) | copy-start | bytes 12292
  188.6 218.8 %copy-start.65 = (s32[2,512]{1,0:T(2,128)}, s32[2,512]{1,0:T(2,128)S(1)}, u32[]{:S(2)}) copy-start(s32[2,512]{1,0:T(2,128)S(1)} %get-tuple-element.86) | copy-start | bytes 12292
  188.6 218.8 %copy-start.67 = (s32[2,512]{1,0:T(2,128)}, s32[2,512]{1,0:T(2,128)S(1)}, u32[]{:S(2)}) copy-start(s32[2,512]{1,0:T(2,128)S(1)} %get-tuple-element.87) | copy-start | bytes 12292
  188.6 218.8 %copy-start.69 = (s32[2,512]{1,0:T(2,128)}, s32[2,512]{1,0:T(2,128)S(1)}, u32[]{:S(2)}) copy-start(s32[2,512]{1,0:T(2,128)S(1)} %get-tuple-element.88) | copy-start | bytes 12292
  188.7 218.7 %copy-start.71 = (s32[2,512]{1,0:T(2,128)}, s32[2,512]{1,0:T(2,128)S(1)}, u32[]{:S(2)}) copy-start(s32[2,512]{1,0:T(2,128)S(1)} %get-tuple-element.89) | copy-start | bytes 12292
  188.7 218.7 %copy-start.73 = (s32[2,512]{1,0:T(2,128)}, s32[2,512]{1,0:T(2,128)S(1)}, u32[]{:S(2)}) copy-start(s32[2,512]{1,0:T(2,128)S(1)} %get-tuple-element.90) | copy-start | bytes 12292
  188.7 218.7 %copy-start.75 = (s32[2,512]{1,0:T(2,128)}, s32[2,512]{1,0:T(2,128)S(1)}, u32[]{:S(2)}) copy-start(s32[2,512]{1,0:T(2,128)S(1)} %get-tuple-element.91) | copy-start | bytes 12292
  188.7 218.7 %copy-start.77 = (s32[2,512]{1,0:T(2,128)}, s32[2,512]{1,0:T(2,128)S(1)}, u32[]{:S(2)}) copy-start(s32[2,512]{1,0:T(2,128)S(1)} %get-tuple-element.92) | copy-start | bytes 12292
  188.8 243.3 %copy-start.40 = (f32[2,1024]{1,0:T(2,128)}, f32[2,1024]{1,0:T(2,128)S(1)}, u32[]{:S(2)}) copy-start(f32[2,1024]{1,0:T(2,128)S(1)} %get-tuple-element.98) | copy-start | bytes 24580
  188.8 243.3 %copy-start.56 = (f32[2,1024]{1,0:T(2,128)}, f32[2,1024]{1,0:T(2,128)S(1)}, u32[]{:S(2)}) copy-start(f32[2,1024]{1,0:T(2,128)S(1)} %get-tuple-element.97) | copy-start | bytes 24580
  188.8 308.5 %copy-start.60 = (f32[2,1024]{1,0:T(2,128)}, f32[2,1024]{1,0:T(2,128)S(1)}, u32[]{:S(2)}) copy-start(f32[2,1024]{1,0:T(2,128)S(1)} %get-tuple-element.95) | copy-start | bytes 24580
  189.8 285.0 %copy-start.2 = (pred[2,512,512]{1,2,0:T(8,128)(4,1)}, pred[2,512,512]{1,2,0:T(8,128)(4,1)S(1)}, u32[]{:S(2)}) copy-start(pred[2,512,512]{1,2,0:T(8,128)(4,1)S(1)} %broadcast_compare_fusion) | copy-start | bytes 1572868
  393.2 38.9 %copy-start.20 = (bf16[6,512,1024]{2,1,0:T(8,128)(2,1)}, bf16[6,512,1024]{2,1,0:T(8,128)(2,1)S(1)}, u32[]{:S(2)}) copy-start(bf16[6,512,1024]{2,1,0:T(8,128)(2,1)S(1)} %slice.160) | copy-start | bytes 18874372
  446.9 13.8 copy-start
  446.9 13.8 copy-start.4
  446.9 28.0 %copy-start.7 = (bf16[1,2,512,1024]{2,3,1,0:T(8,128)(2,1)}, bf16[1,2,512,1024]{2,3,1,0:T(8,128)(2,1)S(1)}, u32[]{:S(2)}) copy-start(bf16[1,2,512,1024]{2,3,1,0:T(8,128)(2,1)S(1)} %get-tuple-element.43) | copy-start | bytes 6291460
  474.8 15.6 copy-start.29
  496.7 50.0 %copy-start.10 = (f32[2,512,1024]{2,1,0:T(8,128)}, f32[2,512,1024]{2,1,0:T(8,128)S(1)}, u32[]{:S(2)}) copy-start(f32[2,512,1024]{2,1,0:T(8,128)S(1)} %get-tuple-element.74) | copy-start | bytes 12582916
  586.1 40.3 %copy-start.8 = (f32[2,512,1024]{2,1,0:T(8,128)}, f32[2,512,1024]{2,1,0:T(8,128)S(1)}, u32[]{:S(2)}) copy-start(f32[2,512,1024]{2,1,0:T(8,128)S(1)} %subtract_multiply_fusion) | copy-start | bytes 12582916
  586.1 24.3 copy-start.11
  636.4 25.8 %copy-start.5 = (bf16[2,512,1024]{1,2,0:T(8,128)(2,1)}, bf16[2,512,1024]{1,2,0:T(8,128)(2,1)S(1)}, u32[]{:S(2)}) copy-start(bf16[2,512,1024]{1,2,0:T(8,128)(2,1)S(1)} %copy.73) | copy-start | bytes 6291460
  662.2 28.4 %copy-start.1 = (bf16[1,2,512,1024]{2,3,1,0:T(8,128)(2,1)S(1)}, bf16[1,2,512,1024]{2,3,1,0:T(8,128)(2,1)}, u32[]{:S(2)}) copy-start(bf16[1,2,512,1024]{2,3,1,0:T(8,128)(2,1)} %copy-done) | copy-start | bytes 6291460
  713.5 16.2 copy-start.61
  729.7 23.3 copy-start.15
  729.7 23.3 copy-start.23
  729.7 23.3 copy-start.37
  729.7 23.3 copy-start.44
  729.7 23.3 copy-start.46
  729.7 23.3 copy-start.59
  729.7 23.3 copy-start.80
  729.7 23.3 copy-start.82
  729.7 23.3 copy-start.102
  760.9 22.9 slice-start.4
  768.9 14.8 copy-start.17
  769.0 14.8 slice-start.5
  769.0 14.8 copy-start.24
  769.0 14.8 copy-start.25
  769.0 14.8 copy-start.26
  794.1 1591.5 %reduce-scatter.2.cloned.1.call-start = ((), (), s32[]{:S(2)}) async-start(), calls=%async_computation.3 | async-start | bytes 69206016 | tf_op jit(solution)/shard_map/reduce_scatter | solution.py:301
  824.9 17.4 slice-start
  829.2 13.1 copy-start.9
  829.2 13.1 slice-start.1
  854.6 21.3 copy-start.62
  982.9 1406.1 %copy-start.99 = (f32[8]{0:T(128)S(1)}, f32[8]{0:T(128)}, u32[]{:S(2)}) copy-start(f32[8]{0:T(128)} %get-tuple-element.22) | copy-start | bytes 100
  982.9 1446.2 %copy-start.108 = (f32[8]{0:T(128)S(1)}, f32[8]{0:T(128)}, u32[]{:S(2)}) copy-start(f32[8]{0:T(128)} %copy-done.107) | copy-start | bytes 100
  982.9 1446.8 %copy-start.32 = (f32[2,6144]{1,0:T(2,128)S(1)}, f32[2,6144]{1,0:T(2,128)}, u32[]{:S(2)}) copy-start(f32[2,6144]{1,0:T(2,128)} %param.16) | copy-start | bytes 147460
  982.9 1446.8 %copy-start.34 = (f32[2,6144]{1,0:T(2,128)S(1)}, f32[2,6144]{1,0:T(2,128)}, u32[]{:S(2)}) copy-start(f32[2,6144]{1,0:T(2,128)} %param.18) | copy-start | bytes 147460
  982.9 1446.8 %copy-start.35 = (f32[2,6144]{1,0:T(2,128)S(1)}, f32[2,6144]{1,0:T(2,128)}, u32[]{:S(2)}) copy-start(f32[2,6144]{1,0:T(2,128)} %param.17) | copy-start | bytes 147460
  982.9 1448.6 %copy-start.19 = (f32[8,64,1024]{2,1,0:T(8,128)S(1)}, f32[8,64,1024]{2,1,0:T(8,128)}, u32[]{:S(2)}) copy-start(f32[8,64,1024]{2,1,0:T(8,128)} %param.13) | copy-start | bytes 6291460
  (55 other events, 351.8 us)
Sparse Core Ops, SparseCore 0:
  10.8 127.5 all-gather.3
  140.0 201.4 all-gather.5
  794.2 123.0 all-reduce.3
  983.0 1402.4 reduce-scatter.1
where the time goes:
time: 2450 us
  waiting for transfers between devices  1680 us (69%)
  matrix products  327 us (13%)
  local copies, waits for them, and re-layouts  239 us (10%)
  other arithmetic  94.4 us (4%)
  blocking collectives  85.5 us (3%)
    reduce_scatter x1, waiting for transfers between devices, per_device(): lax.psum_scatter(arranged, ('section', 'batch'), scatter_dimension=0, til...  1400 us
    all_gather x1, waiting for transfers between devices, per_device(): all_slots = lax.all_gather(shard_rows, 'section', axis=0, tiled=True)  152 us
    all_gather x1, waiting for transfers between devices, per_device(): lax.all_gather(masters.astype(jnp.bfloat16), 'batch', axis=1, tiled=True)  128 us
    scatter x1, local copies, waits for them, and re-layouts, per_device(): arranged.at[target_slot.reshape(-1)]  107 us
    dot_general x1, matrix products, forward(): jnp.einsum('rld,gde->rlge', input_two, up_w, preferred_element_type=float...  49.3 us
  transfers between devices with their start and end apart: 4, of which 3 were waited for; matrix products, arithmetic and copies ran while one was open for 8% of the time, Pallas kernels for 0%

commit v1 on v0

--- a/solution.py
+++ b/solution.py
@@ -23,6 +23,27 @@
 pos_scale = 0.1
 exact = lax.Precision.HIGHEST
 float_out = jnp.float32
+
+
+def joined_along(blocks, dim):
+    blocks = jnp.moveaxis(blocks, 0, dim)
+    shape = blocks.shape
+    return blocks.reshape(*shape[:dim], shape[dim] * shape[dim + 1], *shape[dim + 2 :])
+
+
+def collected_by_bits(x, axis):
+    size, index = (lax.axis_size(axis), lax.axis_index(axis))
+    blocks, distance = (x[None], 1)
+    while distance < size:
+        theirs = lax.ppermute(blocks, axis, [(i, i ^ distance) for i in range(size)])
+        low = index & distance == 0
+        blocks = jnp.concatenate([jnp.where(low, blocks, theirs), jnp.where(low, theirs, blocks)])
+        distance *= 2
+    return blocks
+
+
+def doubled_up(x, axis, dim):
+    return joined_along(collected_by_bits(x, axis), dim)
 
 
 def positions(segs):
@@ -264,7 +285,7 @@
     row_count = section_ids.shape[0]
     section_hot = (section_ids[:, None] == jnp.arange(SECTIONS)[None, :]).astype(jnp.float32)
     local_counts = jnp.sum(section_hot, axis=0) * segments.shape[1]
-    shard_rows = lax.all_gather(masters.astype(jnp.bfloat16), "batch", axis=1, tiled=True)
+    shard_rows = doubled_up(masters.astype(jnp.bfloat16), "batch", 1)
     all_slots = lax.all_gather(shard_rows, "section", axis=0, tiled=True)
     blocks = jnp.take(all_slots, owners, axis=0)
     table = lax.all_gather(section_table, "section", axis=0, tiled=True)

time: 2450 us -> 2600 us (1.061)
  waiting for transfers between devices: 1680 us -> 1800 us
    ppermute x0 -> x3, waiting for transfers between devices: none -> 248 us  [collected_by_bits(): lax.ppermute(blocks, axis, [(i, i ^ distance) for i in range(size)])]
    all_gather x1 -> x0, waiting for transfers between devices: 128 us -> none  [per_device(): lax.all_gather(masters.astype(jnp.bfloat16), 'batch', axis=1, tiled=True)]
  transfers between devices with their start and end apart: 4 -> 6, of which waited for: 3 -> 5; matrix products, arithmetic and copies ran while one was open for 8% -> 7% of each run, Pallas kernels for 0% -> 0%
where the time goes in v1:
time: 2600 us; the launch traced here: 2590 us
  waiting for transfers between devices  1800 us (69%)
  matrix products  327 us (13%)
  local copies, waits for them, and re-layouts  240 us (9%)
  other arithmetic  113 us (4%)
  blocking collectives  86.5 us (3%)
    reduce_scatter x1, waiting for transfers between devices, per_device(): lax.psum_scatter(arranged, ('section', 'batch'), scatter_dimension=0, til...  1400 us
    ppermute x3, waiting for transfers between devices, collected_by_bits(): lax.ppermute(blocks, axis, [(i, i ^ distance) for i in range(size)])  248 us
    all_gather x1, waiting for transfers between devices, per_device(): all_slots = lax.all_gather(shard_rows, 'section', axis=0, tiled=True)  152 us
    scatter x1, local copies, waits for them, and re-layouts, per_device(): arranged.at[target_slot.reshape(-1)]  107 us
  transfers between devices with their start and end apart: 6, of which 5 were waited for; matrix products, arithmetic and copies ran while one was open for 7% of the time, Pallas kernels for 0%

profile of v1, /device:TPU:0, one launch (start us, length us, event | category | flops | bytes accessed | tf_op | source)
XLA Modules:
  0.0 2593.5 jit_solution(3504954028603516643)
XLA Ops:
  9.1 3.0 collective-permute-start
  12.1 23.3 collective-permute-done
  38.0 1.9 collective-permute-start.1
  39.9 45.1 %collective-permute-done.1 = bf16[2,8,64,1024]{3,2,0,1:T(8,128)(2,1)} collective-permute-done((bf16[2,8,64,1024]{3,2,0,1:T(8,128)(2,1)S(1)}, bf16[2,8,64,1024]{3,2,0,1:T(8,128)(2,1)}, u32[]{:S(2)}, u32[]{:S(2)}) %collective-permute-start.1) | collective-permute-done | bytes 2097184 | tf_op jit(solution)/shard_map/ppermute | solution.py:38
  85.0 2.1 broadcast_select_fusion.4
  87.1 2.6 pad_maximum_fusion.2
  89.8 2.5 collective-permute-start.2
  92.3 179.4 %collective-permute-done.2 = bf16[4,8,64,1024]{3,2,0,1:T(8,128)(2,1)} collective-permute-done((bf16[4,8,64,1024]{3,2,0,1:T(8,128)(2,1)}, bf16[4,8,64,1024]{3,2,0,1:T(8,128)(2,1)}, u32[]{:S(2)}, u32[]{:S(2)}) %collective-permute-start.2) | collective-permute-done | bytes 4194336 | tf_op jit(solution)/shard_map/ppermute | solution.py:38
  271.7 5.4 broadcast_select_fusion.2
  277.2 7.4 pad_maximum_fusion
  285.4 39.7 %psum.28 = f32[8]{0:T(128)S(1)} all-reduce(f32[8]{0:T(128)S(1)} %broadcast_multiply_fusion.10), channel_id=1, replica_groups=mesh['section'=4,'batch'=8] {'section','batch'}, use_global_device_ids=true, to_apply=%region_13.14 | all-reduce | flops 8 | bytes 64 | tf_op jit(solution)/shard_map/psum | solution.py:299
  326.3 7.4 all-gather
  337.0 151.8 %all-gather.3.cloned.1.call-done = bf16[32,512,1024]{2,1,0:T(8,128)(2,1)} async-done(((bf16[8,512,1024]{2,1,0:T(8,128)(2,1)}), bf16[32,512,1024]{2,1,0:T(8,128)(2,1)}) %all-gather.3.cloned.1.call-update) | async-done | bytes 33554448 | tf_op jit(solution)/shard_map/all_gather | solution.py:289
  488.8 22.0 gather_fusion
  510.9 20.5 broadcast_select_fusion
  531.4 5.7 fusion.89
  537.1 3.5 slice.160
  540.6 14.0 fusion.88
  554.8 6.3 fusion.82
  561.1 17.8 fusion.92
  580.7 10.1 convert_bitcast_fusion
  590.8 3.3 fusion.90
  594.1 13.7 fusion
  607.9 14.1 exponential_reduce_fusion
  622.1 15.6 convolution_convert_fusion.2
  637.7 6.3 fusion.93
  644.6 49.3 %multiply_convert_fusion.1 = (bf16[2,512,4,1024]{3,1,2,0:T(8,128)(2,1)}, f32[2,512,4,1024]{3,1,2,0:T(8,128)}, f32[2,512,4,1024]{3,1,2,0:T(8,128)}) fusion(bf16[4,1024,1024,1]{2,1,0,3:T(8,128)(2,1)S(1)} %bitcast.266, f32[2,512,1024]{2,1,0:T(8,128)S(1)} %get-tuple-element.80, f32[2,1024]{1,0:T(2,128)S(1)} %get-tuple-element.101, ...), kind=kOutput, calls=%fused_computation.14 | convolution fusion | flops 8867807232 | bytes 54550528 | tf_op jit(solution)/shard_map/rld,gde->rlge/dot_general | solution.py:137
  693.9 11.4 copy.71
  705.3 14.7 fusion.94
  720.6 2.5 copy-done.31
  723.1 2.5 fusion.95
  728.1 4.0 multiply_reduce_fusion.1
  733.3 24.3 add_convert_fusion
  757.6 16.0 fusion.12
  775.0 2.1 copy-done.15
  777.1 3.7 convolution_convert_fusion.1
  780.8 2.9 copy.73
  783.7 25.7 multiply_reduce_fusion
  809.4 28.4 %multiply_convert_fusion = bf16[2,16,512,512]{2,3,1,0:T(8,128)(2,1)} fusion(f32[2,16,512,512]{2,3,1,0:T(8,128)} %get-tuple-element.89, f32[2,16,512,512]{2,3,1,0:T(8,128)} %get-tuple-element.78, f32[2,16,512]{2,1,0:T(8,128)S(1)} %get-tuple-element.88, f32[2,16,512]{2,1,0:T(8,128)S(1)} %copy-done.33, pred[2,512,512]{1,2,0:T(8,128)(4,1)S(1)} %copy-done.3), kind=kLoop, calls=%fused_computation.2 | loop fusion | flops 50331648 | bytes 84541440 | tf_op jit(solution)/shard_map/convert_element_type | solution.py:230
  837.8 9.9 multiply_convert_fusion.3
  847.7 13.0 multiply_convert_fusion.2
  860.7 16.2 convolution_convert_fusion
  877.0 23.3 fusion.76
  900.3 5.4 fusion.49
  905.7 2.4 copy.77
  908.2 4.1 copy.78
  912.3 3.9 copy.79
  916.2 14.8 fusion.23
  931.1 9.2 fusion.11
  941.6 5.5 add_convert_fusion.1
  947.3 5.5 fusion.80
  952.9 2.3 constant_dynamic-update-slice_fusion.3
  955.2 2.6 bitcast_dynamic-update-slice_fusion.2
  957.8 2.3 constant_dynamic-update-slice_fusion.2
  960.1 12.1 constant_dynamic-update-slice_fusion.1
  972.2 4.3 bitcast_dynamic-update-slice_fusion.1
  976.5 13.1 constant_dynamic-update-slice_fusion
  989.6 12.3 bitcast_dynamic-update-slice_fusion
  1001.9 21.3 broadcast_in_dim.46
  1023.2 106.9 %scatter_fusion = f32[256,64,1024]{2,1,0:T(8,128)} fusion(f32[256,64,1024]{2,1,0:T(8,128)} %broadcast_in_dim.46, s32[232]{0:T(256)S(1)} %bitcast.288, f32[232,64,1024]{2,1,0:T(8,128)} %bitcast.245), kind=kCustom, calls=%fused_computation.1 | custom fusion | bytes 182453152 | tf_op jit(solution)/shard_map/scatter | solution.py:321
  1133.3 1399.5 %reduce-scatter.2.cloned.1.call-done = f32[8,64,1024]{2,1,0:T(8,128)} async-done(((f32[256,64,1024]{2,1,0:T(8,128)}), f32[8,64,1024]{2,1,0:T(8,128)}) %reduce-scatter.2.cloned.1.call-update) | async-done | bytes 2097168 | tf_op jit(solution)/shard_map/reduce_scatter | solution.py:322
  2532.8 2.7 multiply_reduce_fusion.9
  2536.2 39.4 %all-reduce.1 = (f32[]{:T(128)}, f32[8]{0:T(128)S(1)}) all-reduce(f32[]{:T(128)S(6)} %add.310, f32[8]{0:T(128)S(1)} %copy-done.102), channel_id=1, replica_groups=mesh['section'=4,'batch'=8] {'section','batch'}, use_global_device_ids=true, to_apply=%region_33.34 | all-reduce | flops 9 | bytes 72 | tf_op jit(solution)/shard_map/psum | solution.py:324
  2578.7 6.9 multiply_subtract_fusion
  (315 shorter events, 22.9 us)
Async XLA Ops:
  7.2 28.2 %copy-start.5 = (f32[8,64,1024]{2,1,0:T(8,128)S(1)}, f32[8,64,1024]{2,1,0:T(8,128)}, u32[]{:S(2)}) copy-start(f32[8,64,1024]{2,1,0:T(8,128)} %param.13) | copy-start | bytes 6291460
  7.2 481.7 %all-gather.3.cloned.1.call-start = ((), (), s32[]{:S(2)}) async-start(), calls=%async_computation.1 | async-start | bytes 41943040 | tf_op jit(solution)/shard_map/all_gather | solution.py:289
  9.1 26.3 %collective-permute-start = (bf16[1,8,64,1024]{3,2,0,1:T(8,128)(2,1)S(1)}, bf16[1,8,64,1024]{3,2,0,1:T(8,128)(2,1)}, u32[]{:S(2)}, u32[]{:S(2)}) collective-permute-start(bf16[1,8,64,1024]{3,2,0,1:T(8,128)(2,1)S(1)} %convert_bitcast_fusion.1), channel_id=1, source_target_pairs={{0,1},{1,0},{2,3},{3,2},{4,5},{5,4},{6,7},{7,6},{8,9},{9,8},{10,11... | collective-permute-start | bytes 3145736 | tf_op jit(solution)/shard_map/ppermute | solution.py:38
  38.0 47.0 %collective-permute-start.1 = (bf16[2,8,64,1024]{3,2,0,1:T(8,128)(2,1)S(1)}, bf16[2,8,64,1024]{3,2,0,1:T(8,128)(2,1)}, u32[]{:S(2)}, u32[]{:S(2)}) collective-permute-start(bf16[2,8,64,1024]{3,2,0,1:T(8,128)(2,1)S(1)} %pad_maximum_fusion.5), channel_id=1, source_target_pairs={{0,2},{1,3},{2,0},{3,1},{4,6},{5,7},{6,4},{7,5},{8,10},{9,11},{10,... | collective-permute-start | bytes 6291464 | tf_op jit(solution)/shard_map/ppermute | solution.py:38
  89.8 181.9 %collective-permute-start.2 = (bf16[4,8,64,1024]{3,2,0,1:T(8,128)(2,1)}, bf16[4,8,64,1024]{3,2,0,1:T(8,128)(2,1)}, u32[]{:S(2)}, u32[]{:S(2)}) collective-permute-start(bf16[4,8,64,1024]{3,2,0,1:T(8,128)(2,1)} %pad_maximum_fusion.2), channel_id=1, source_target_pairs={{0,4},{1,5},{2,6},{3,7},{4,0},{5,1},{6,2},{7,3},{8,12},{9,13},{10,... | collective-permute-start | bytes 12582920 | tf_op jit(solution)/shard_map/ppermute | solution.py:38
  284.6 40.5 %copy-start.36 = (s32[2,512]{1,0:T(2,128)S(1)}, s32[2,512]{1,0:T(2,128)}, u32[]{:S(2)}) copy-start(s32[2,512]{1,0:T(2,128)} %param.23) | copy-start | bytes 12292
  284.6 41.7 %copy-start.34 = (f32[2,6144]{1,0:T(2,128)S(1)}, f32[2,6144]{1,0:T(2,128)}, u32[]{:S(2)}) copy-start(f32[2,6144]{1,0:T(2,128)} %param.16) | copy-start | bytes 147460
  284.6 49.6 %copy-start.106 = (s32[29]{0:T(128)S(1)}, s32[29]{0:T(128)}, u32[]{:S(2)}) copy-start(s32[29]{0:T(128)} %param.19) | copy-start | bytes 352
  284.6 51.1 %copy-start.45 = (s32[2,512,8]{1,2,0:T(8,128)S(1)}, s32[2,512,8]{1,2,0:T(8,128)}, u32[]{:S(2)}) copy-start(s32[2,512,8]{1,2,0:T(8,128)} %param.22) | copy-start | bytes 98308
  284.6 846.4 %all-reduce.4.cloned.1.call-start = ((), (), s32[]{:S(2)}) async-start(), calls=%async_computation.3 | async-start | bytes 393216 | tf_op jit(solution)/shard_map/psum | solution.py:305
  335.6 219.1 %copy-start.86 = (bf16[2]{0:T(256)(128)(2,1)}, bf16[2]{0:T(256)(128)(2,1)S(1)}, u32[]{:S(2)}) copy-start(bf16[2]{0:T(256)(128)(2,1)S(1)} %get-tuple-element.64) | copy-start | bytes 16
  335.6 219.1 %copy-start.88 = (bf16[2]{0:T(256)(128)(2,1)}, bf16[2]{0:T(256)(128)(2,1)S(1)}, u32[]{:S(2)}) copy-start(bf16[2]{0:T(256)(128)(2,1)S(1)} %get-tuple-element.65) | copy-start | bytes 16
  335.6 219.1 %copy-start.90 = (bf16[2]{0:T(256)(128)(2,1)}, bf16[2]{0:T(256)(128)(2,1)S(1)}, u32[]{:S(2)}) copy-start(bf16[2]{0:T(256)(128)(2,1)S(1)} %get-tuple-element.66) | copy-start | bytes 16
  335.6 219.1 %copy-start.92 = (bf16[2]{0:T(256)(128)(2,1)}, bf16[2]{0:T(256)(128)(2,1)S(1)}, u32[]{:S(2)}) copy-start(bf16[2]{0:T(256)(128)(2,1)S(1)} %get-tuple-element.67) | copy-start | bytes 16
  335.6 219.1 %copy-start.94 = (bf16[2]{0:T(256)(128)(2,1)}, bf16[2]{0:T(256)(128)(2,1)S(1)}, u32[]{:S(2)}) copy-start(bf16[2]{0:T(256)(128)(2,1)S(1)} %get-tuple-element.68) | copy-start | bytes 16
  335.6 219.1 %copy-start.96 = (bf16[2]{0:T(256)(128)(2,1)}, bf16[2]{0:T(256)(128)(2,1)S(1)}, u32[]{:S(2)}) copy-start(bf16[2]{0:T(256)(128)(2,1)S(1)} %get-tuple-element.69) | copy-start | bytes 16
  335.6 219.1 %copy-start.98 = (bf16[2]{0:T(256)(128)(2,1)}, bf16[2]{0:T(256)(128)(2,1)S(1)}, u32[]{:S(2)}) copy-start(bf16[2]{0:T(256)(128)(2,1)S(1)} %get-tuple-element.70) | copy-start | bytes 16
  335.6 219.1 %copy-start.100 = (bf16[2]{0:T(256)(128)(2,1)}, bf16[2]{0:T(256)(128)(2,1)S(1)}, u32[]{:S(2)}) copy-start(bf16[2]{0:T(256)(128)(2,1)S(1)} %get-tuple-element.71) | copy-start | bytes 16
  335.8 218.9 %copy-start.66 = (s32[2,512]{1,0:T(2,128)}, s32[2,512]{1,0:T(2,128)S(1)}, u32[]{:S(2)}) copy-start(s32[2,512]{1,0:T(2,128)S(1)} %get-tuple-element.91) | copy-start | bytes 12292
  335.8 218.9 %copy-start.68 = (s32[2,512]{1,0:T(2,128)}, s32[2,512]{1,0:T(2,128)S(1)}, u32[]{:S(2)}) copy-start(s32[2,512]{1,0:T(2,128)S(1)} %get-tuple-element.92) | copy-start | bytes 12292
  335.8 218.9 %copy-start.70 = (s32[2,512]{1,0:T(2,128)}, s32[2,512]{1,0:T(2,128)S(1)}, u32[]{:S(2)}) copy-start(s32[2,512]{1,0:T(2,128)S(1)} %get-tuple-element.93) | copy-start | bytes 12292
  335.8 218.9 %copy-start.72 = (s32[2,512]{1,0:T(2,128)}, s32[2,512]{1,0:T(2,128)S(1)}, u32[]{:S(2)}) copy-start(s32[2,512]{1,0:T(2,128)S(1)} %get-tuple-element.94) | copy-start | bytes 12292
  335.9 218.9 %copy-start.74 = (s32[2,512]{1,0:T(2,128)}, s32[2,512]{1,0:T(2,128)S(1)}, u32[]{:S(2)}) copy-start(s32[2,512]{1,0:T(2,128)S(1)} %get-tuple-element.95) | copy-start | bytes 12292
  335.9 218.9 %copy-start.76 = (s32[2,512]{1,0:T(2,128)}, s32[2,512]{1,0:T(2,128)S(1)}, u32[]{:S(2)}) copy-start(s32[2,512]{1,0:T(2,128)S(1)} %get-tuple-element.96) | copy-start | bytes 12292
  335.9 218.9 %copy-start.78 = (s32[2,512]{1,0:T(2,128)}, s32[2,512]{1,0:T(2,128)S(1)}, u32[]{:S(2)}) copy-start(s32[2,512]{1,0:T(2,128)S(1)} %get-tuple-element.97) | copy-start | bytes 12292
  335.9 218.9 %copy-start.80 = (s32[2,512]{1,0:T(2,128)}, s32[2,512]{1,0:T(2,128)S(1)}, u32[]{:S(2)}) copy-start(s32[2,512]{1,0:T(2,128)S(1)} %get-tuple-element.98) | copy-start | bytes 12292
  336.0 243.5 %copy-start.43 = (f32[2,1024]{1,0:T(2,128)}, f32[2,1024]{1,0:T(2,128)S(1)}, u32[]{:S(2)}) copy-start(f32[2,1024]{1,0:T(2,128)S(1)} %get-tuple-element.104) | copy-start | bytes 24580
  336.0 243.5 %copy-start.59 = (f32[2,1024]{1,0:T(2,128)}, f32[2,1024]{1,0:T(2,128)S(1)}, u32[]{:S(2)}) copy-start(f32[2,1024]{1,0:T(2,128)S(1)} %get-tuple-element.103) | copy-start | bytes 24580
  336.0 308.5 %copy-start.63 = (f32[2,1024]{1,0:T(2,128)}, f32[2,1024]{1,0:T(2,128)S(1)}, u32[]{:S(2)}) copy-start(f32[2,1024]{1,0:T(2,128)S(1)} %get-tuple-element.101) | copy-start | bytes 24580
  337.0 285.1 %copy-start.2 = (pred[2,512,512]{1,2,0:T(8,128)(4,1)}, pred[2,512,512]{1,2,0:T(8,128)(4,1)S(1)}, u32[]{:S(2)}) copy-start(pred[2,512,512]{1,2,0:T(8,128)(4,1)S(1)} %broadcast_compare_fusion) | copy-start | bytes 1572868
  540.6 38.9 %copy-start.23 = (bf16[6,512,1024]{2,1,0:T(8,128)(2,1)}, bf16[6,512,1024]{2,1,0:T(8,128)(2,1)S(1)}, u32[]{:S(2)}) copy-start(bf16[6,512,1024]{2,1,0:T(8,128)(2,1)S(1)} %slice.160) | copy-start | bytes 18874372
  594.1 13.8 copy-start
  594.1 28.0 %copy-start.10 = (bf16[1,2,512,1024]{2,3,1,0:T(8,128)(2,1)}, bf16[1,2,512,1024]{2,3,1,0:T(8,128)(2,1)S(1)}, u32[]{:S(2)}) copy-start(bf16[1,2,512,1024]{2,3,1,0:T(8,128)(2,1)S(1)} %get-tuple-element.45) | copy-start | bytes 6291460
  622.1 15.6 copy-start.32
  644.0 49.9 %copy-start.13 = (f32[2,512,1024]{2,1,0:T(8,128)}, f32[2,512,1024]{2,1,0:T(8,128)S(1)}, u32[]{:S(2)}) copy-start(f32[2,512,1024]{2,1,0:T(8,128)S(1)} %get-tuple-element.80) | copy-start | bytes 12582916
  733.3 40.3 %copy-start.11 = (f32[2,512,1024]{2,1,0:T(8,128)}, f32[2,512,1024]{2,1,0:T(8,128)S(1)}, u32[]{:S(2)}) copy-start(f32[2,512,1024]{2,1,0:T(8,128)S(1)} %subtract_multiply_fusion) | copy-start | bytes 12582916
  733.3 24.3 copy-start.14
  783.7 25.7 copy-start.8
  809.4 28.4 %copy-start.1 = (bf16[1,2,512,1024]{2,3,1,0:T(8,128)(2,1)S(1)}, bf16[1,2,512,1024]{2,3,1,0:T(8,128)(2,1)}, u32[]{:S(2)}) copy-start(bf16[1,2,512,1024]{2,3,1,0:T(8,128)(2,1)} %copy-done) | copy-start | bytes 6291460
  860.7 16.2 copy-start.64
  876.9 23.4 copy-start.18
  876.9 23.4 copy-start.26
  876.9 23.4 copy-start.40
  876.9 23.4 copy-start.47
  876.9 23.4 copy-start.49
  876.9 23.4 copy-start.62
  876.9 23.4 copy-start.83
  876.9 23.4 copy-start.85
  877.0 23.4 copy-start.105
  908.2 22.9 slice-start.4
  916.2 14.8 copy-start.20
  916.2 14.8 slice-start.5
  916.2 14.8 copy-start.27
  916.2 14.8 copy-start.28
  916.2 14.8 copy-start.29
  941.4 1591.4 %reduce-scatter.2.cloned.1.call-start = ((), (), s32[]{:S(2)}) async-start(), calls=%async_computation.2 | async-start | bytes 69206016 | tf_op jit(solution)/shard_map/reduce_scatter | solution.py:322
  972.2 17.4 slice-start
  1001.9 21.3 copy-start.65
  1130.1 1406.1 %copy-start.102 = (f32[8]{0:T(128)S(1)}, f32[8]{0:T(128)}, u32[]{:S(2)}) copy-start(f32[8]{0:T(128)} %get-tuple-element.22) | copy-start | bytes 100
  1130.1 1446.1 %copy-start.111 = (f32[8]{0:T(128)S(1)}, f32[8]{0:T(128)}, u32[]{:S(2)}) copy-start(f32[8]{0:T(128)} %copy-done.110) | copy-start | bytes 100
  1130.1 1446.8 %copy-start.35 = (f32[2,6144]{1,0:T(2,128)S(1)}, f32[2,6144]{1,0:T(2,128)}, u32[]{:S(2)}) copy-start(f32[2,6144]{1,0:T(2,128)} %param.16) | copy-start | bytes 147460
  1130.1 1446.8 %copy-start.37 = (f32[2,6144]{1,0:T(2,128)S(1)}, f32[2,6144]{1,0:T(2,128)}, u32[]{:S(2)}) copy-start(f32[2,6144]{1,0:T(2,128)} %param.18) | copy-start | bytes 147460
  1130.1 1446.8 %copy-start.38 = (f32[2,6144]{1,0:T(2,128)S(1)}, f32[2,6144]{1,0:T(2,128)}, u32[]{:S(2)}) copy-start(f32[2,6144]{1,0:T(2,128)} %param.17) | copy-start | bytes 147460
  1130.1 1448.6 %copy-start.6 = (f32[8,64,1024]{2,1,0:T(8,128)S(1)}, f32[8,64,1024]{2,1,0:T(8,128)}, u32[]{:S(2)}) copy-start(f32[8,64,1024]{2,1,0:T(8,128)} %param.13) | copy-start | bytes 6291460
  (60 other events, 395.0 us)
Sparse Core Ops, SparseCore 0:
  284.8 204.0 all-gather.2
  941.5 123.0 all-reduce.3
  1130.3 1402.4 reduce-scatter.1
